TPU v7x, 32 devices: a whole 2x2x4 slice. The times are simulated.
32 devices in a mesh: gx: 4 (over y, core), gy: 8 (over z, x).
Axes of the slice: x: 2, y: 2, z: 4, core: 2. Of those that a mesh axis runs over, the one named last changes fastest.
Arguments:
- perturbation: float32 [5, 16, 512], P(None, 'gx', 'gy'), may hold values from -6 to 6
- mean_velocity: float32 [16, 512], P('gx', 'gy'), may hold values from 0.2 to 0.9
- mean_shear: float32 [16, 512], P('gx', 'gy'), may hold values from -4 to 4
- cotangent: float32 [5, 16, 512], P(None, 'gx', 'gy'), may hold values from -6 to 6
- kernel_in: bfloat16 [64, 135], replicated, may hold values from -0.5 to 0.5
- kernel_mid: bfloat16 [64, 1728], replicated, may hold values from -0.15625 to 0.15625
- kernel_out: bfloat16 [5, 1728], replicated, may hold values from -0.15625 to 0.15625
Outputs:
- advanced: float32 [5, 16, 512], P(None, 'gx', 'gy')
- grad_in: float32 [64, 135], replicated
- grad_mid: float32 [64, 1728], replicated
- grad_out: float32 [5, 1728], replicated
All inputs are finite; a program needn't handle non-finite values.
Results may differ from a plain program's by a relative error of at most 0.0065.
Values may be sent and summed in bfloat16 or wider, within the bound.
A program may use at most 64 MiB of HBM per device.

v0:
```python
import math
import jax
import jax.numpy as jnp
from jax import lax
from jax.sharding import PartitionSpec as P

NZ = 8
STEPS = 2
TIME_STEP = 0.25
STENCIL_WEIGHTS = (0.75, -0.15, 1.0 / 60.0)


def padded_2(cells, sides, width):
    for axis, dim in sides:
        count = lax.axis_size(axis)
        ends = count - 1
        head = lax.slice_in_dim(cells, 0, width, axis=dim)
        tail = lax.slice_in_dim(cells, cells.shape[dim] - width, cells.shape[dim], axis=dim)
        cells = jnp.concatenate(
            [
                lax.ppermute(tail, axis, [(i, (i + 1) % count) for i in range(ends)]),
                cells,
                lax.ppermute(head, axis, [((i + 1) % count, i) for i in range(ends)]),
            ],
            axis=dim,
        )
    return cells


def wrap_depth(grid_field, margin):
    size_z = grid_field.shape[3]
    return jnp.concatenate(
        [grid_field[:, :, :, size_z - margin :], grid_field, grid_field[:, :, :, :margin]], axis=3
    )


def difference(padded, direction, margin, length):
    summed = None
    for offset, weight in zip((1, 2, 3), STENCIL_WEIGHTS):
        upper_cells = lax.slice_in_dim(
            padded, margin + offset, margin + offset + length, axis=direction
        )
        lower_cells = lax.slice_in_dim(
            padded, margin - offset, margin - offset + length, axis=direction
        )
        contrib = weight * (upper_cells - lower_cells)
        summed = contrib if summed is None else summed + contrib
    return summed


def rates_from(padded, margin, velocity, shear_rate):
    size_x = padded.shape[1] - 2 * margin
    size_y = padded.shape[2] - 2 * margin
    interior = padded[:, margin : margin + size_x, margin : margin + size_y]
    slope_x = difference(padded[:, :, margin : margin + size_y], 1, margin, size_x)
    slope_y = difference(padded[:, margin : margin + size_x], 2, margin, size_y)
    slope_z = difference(wrap_depth(interior, 3), 3, 3, interior.shape[3])
    divergence = slope_x[1] + slope_y[2] + slope_z[3]
    return jnp.stack(
        [
            -velocity * slope_x[0] - divergence,
            -velocity * slope_x[1] - shear_rate * interior[2] - slope_x[4],
            -velocity * slope_x[2] - slope_y[4],
            -velocity * slope_x[3] - slope_z[4],
            -velocity * slope_x[4] - divergence,
        ]
    )


def adjoint_fields(adjoint_in, velocity):
    acoustic = adjoint_in[0] + adjoint_in[4]
    return jnp.stack(
        [
            velocity * adjoint_in[0],
            velocity * adjoint_in[1] + acoustic,
            velocity * adjoint_in[2],
            velocity * adjoint_in[3],
            velocity * adjoint_in[4] + adjoint_in[1],
            acoustic,
            adjoint_in[2],
            adjoint_in[3],
        ]
    )


def adjoint_from(padded, margin, adjoint_in, shear_rate):
    size_x = padded.shape[1] - 2 * margin
    size_y = padded.shape[2] - 2 * margin
    interior = padded[:, margin : margin + size_x, margin : margin + size_y]
    slope_x = difference(padded[:5, :, margin : margin + size_y], 1, margin, size_x)
    slope_y = difference(padded[5:, margin : margin + size_x], 2, margin, size_y)
    slope_z = difference(wrap_depth(interior[5:], 3), 3, 3, interior.shape[3])
    return jnp.stack(
        [
            slope_x[0],
            slope_x[1],
            slope_x[2] - shear_rate * adjoint_in[1] + slope_y[0],
            slope_x[3] + slope_z[0],
            slope_x[4] + slope_y[1] + slope_z[2],
        ]
    )


def conv_valid(padded, kernel):
    return lax.conv_general_dilated(
        padded[None],
        kernel,
        (1, 1, 1),
        "VALID",
        dimension_numbers=("NCDHW", "OIDHW", "NCDHW"),
        preferred_element_type=jnp.float32,
    )[0]


def flip_kernel(kernel):
    return jnp.transpose(jnp.flip(kernel, (2, 3, 4)), (1, 0, 2, 3, 4))


def kernel_grad(padded, gradient):
    channels = padded.shape[0]
    size_x, size_y, size_z = (gradient.shape[1], gradient.shape[2], gradient.shape[3])
    flat_grad = gradient.reshape(gradient.shape[0], -1)
    pieces = []
    for shift_x in range(3):
        for shift_y in range(3):
            for shift_z in range(3):
                window = padded[
                    :,
                    shift_x : shift_x + size_x,
                    shift_y : shift_y + size_y,
                    shift_z : shift_z + size_z,
                ]
                pieces.append(
                    lax.dot_general(
                        flat_grad,
                        window.reshape(channels, -1),
                        (((1,), (1,)), ((), ())),
                        preferred_element_type=jnp.float32,
                    )
                )
    stacked = jnp.stack(pieces)
    return jnp.transpose(stacked, (1, 2, 0)).reshape(gradient.shape[0], channels * 27)


def closure_backward(saved, source_grad, kernels, need_input, padding_fn):
    kernel_in, kernel_mid, kernel_out = kernels
    padded_in, hidden_one, padded_one, hidden_two, padded_two = saved
    error_out = source_grad.astype(jnp.bfloat16)
    grad_out = kernel_grad(padded_two, error_out)
    back_mid = conv_valid(padding_fn(error_out), flip_kernel(kernel_out)) * (
        1.0 - jnp.square(hidden_two.astype(jnp.float32))
    )
    error_mid = back_mid.astype(jnp.bfloat16)
    grad_mid = kernel_grad(padded_one, error_mid)
    back_in = conv_valid(padding_fn(error_mid), flip_kernel(kernel_mid)) * (
        1.0 - jnp.square(hidden_one.astype(jnp.float32))
    )
    error_in = back_in.astype(jnp.bfloat16)
    grad_in = kernel_grad(padded_in, error_in)
    state_grad = conv_valid(padding_fn(error_in), flip_kernel(kernel_in)) if need_input else None
    return ((grad_in, grad_mid, grad_out), state_grad)


def retreat(adjoint_in, adjoint_fn):
    into_second = 2.0 / 3.0 * adjoint_in + 2.0 / 3.0 * TIME_STEP * adjoint_fn(adjoint_in)
    direct = 1.0 / 3.0 * adjoint_in
    into_first = 0.25 * into_second + 0.25 * TIME_STEP * adjoint_fn(into_second)
    direct = direct + 0.75 * into_second
    carried = direct + into_first + TIME_STEP * adjoint_fn(into_first)
    source_grad = TIME_STEP * (2.0 / 3.0 * adjoint_in + 0.25 * into_second + into_first)
    return (carried, source_grad)


def grad_pad(grid_field):
    return wrap_depth(padded_2(grid_field, (("gx", 1), ("gy", 2)), 1), 1)


def inside(size_x, size_y, margin):
    start_x = lax.axis_index("gx") * size_x - margin
    start_y = lax.axis_index("gy") * size_y - margin
    index_x = start_x + jnp.arange(size_x + 2 * margin, dtype=jnp.int32)
    index_y = start_y + jnp.arange(size_y + 2 * margin, dtype=jnp.int32)
    valid_x = (index_x >= 0) & (index_x < size_x * lax.axis_size("gx"))
    valid_y = (index_y >= 0) & (index_y < size_y * lax.axis_size("gy"))
    return (valid_x[:, None] & valid_y[None, :]).astype(jnp.float32)[None, :, :, None]


def closure_deep(grid_field, kernels):
    kernel_in, kernel_mid, kernel_out = kernels
    size_x, size_y = (grid_field.shape[1], grid_field.shape[2])
    extended = padded_2(grid_field, (("gx", 1), ("gy", 2)), 3)
    input_wide = extended.astype(jnp.bfloat16)
    hidden_wide = (
        jnp.tanh(conv_valid(wrap_depth(input_wide, 1), kernel_in)) * inside(size_x, size_y, 2)
    ).astype(jnp.bfloat16)
    second_wide = (
        jnp.tanh(conv_valid(wrap_depth(hidden_wide, 1), kernel_mid)) * inside(size_x, size_y, 1)
    ).astype(jnp.bfloat16)
    source = conv_valid(wrap_depth(second_wide, 1), kernel_out)
    saved = (
        wrap_depth(input_wide[:, 2:-2, 2:-2], 1),
        hidden_wide[:, 2:-2, 2:-2],
        wrap_depth(hidden_wide[:, 1:-1, 1:-1], 1),
        second_wide[:, 1:-1, 1:-1],
        wrap_depth(second_wide, 1),
    )
    return (extended, source, saved)


def body(perturbation, mean_velocity, mean_shear, cotangent, kernel_in, kernel_mid, kernel_out):
    channels = perturbation.shape[0]
    hidden = kernel_in.shape[0]
    size_x = perturbation.shape[1]
    size_y = perturbation.shape[2] // NZ
    current = perturbation.reshape(channels, size_x, size_y, NZ)
    velocity = mean_velocity.reshape(size_x, size_y, NZ)
    shear_rate = mean_shear.reshape(size_x, size_y, NZ)
    kernels = (
        kernel_in.reshape(hidden, channels, 3, 3, 3),
        kernel_mid.reshape(hidden, hidden, 3, 3, 3),
        kernel_out.reshape(channels, hidden, 3, 3, 3),
    )

    def section_rates(grid_field):
        padded = padded_2(grid_field, (("gx", 1), ("gy", 2)), 3)
        return rates_from(padded, 3, velocity, shear_rate)

    def adjoint_rates(adjoint_in):
        padded = padded_2(adjoint_fields(adjoint_in, velocity), (("gx", 1), ("gy", 2)), 3)
        return adjoint_from(padded, 3, adjoint_in, shear_rate)

    def evaluate(grid_field, with_rates):
        extended, source, saved = closure_deep(grid_field, kernels)
        rate_field = rates_from(extended, 3, velocity, shear_rate) if with_rates else None
        return (source, saved, rate_field)

    history = []
    stored = []
    for step_index in range(STEPS):
        source, saved, rate_field = evaluate(current, True)
        history.append(current)
        stored.append(saved)
        section_one = current + TIME_STEP * (rate_field + source)
        section_two = 0.75 * current + 0.25 * (
            section_one + TIME_STEP * (section_rates(section_one) + source)
        )
        current = 1.0 / 3.0 * current + 2.0 / 3.0 * (
            section_two + TIME_STEP * (section_rates(section_two) + source)
        )
    cell_count = size_x * lax.axis_size("gx") * size_y * lax.axis_size("gy") * NZ
    adjoint_in = cotangent.reshape(channels, size_x, size_y, NZ) * (1.0 / math.sqrt(cell_count))
    totals = None
    for step_index in reversed(range(STEPS)):
        carried, source_grad = retreat(adjoint_in, adjoint_rates)
        saved = evaluate(history[step_index], False)[1]
        kernel_grads, state_grad = closure_backward(
            saved, source_grad, kernels, step_index > 0, grad_pad
        )
        totals = (
            kernel_grads
            if totals is None
            else tuple((sum_old + sum_new for sum_old, sum_new in zip(totals, kernel_grads)))
        )
        if step_index > 0:
            adjoint_in = carried + state_grad
    result = lax.psum((totals[0], totals[1], totals[2]), ("gx", "gy"))
    return (current.reshape(channels, size_x, size_y * NZ), result[0], result[1], result[2])


def solution(mesh):
    return jax.shard_map(
        body,
        mesh=mesh,
        in_specs=(
            P(None, "gx", "gy"),
            P("gx", "gy"),
            P("gx", "gy"),
            P(None, "gx", "gy"),
            P(),
            P(),
            P(),
        ),
        out_specs=(P(None, "gx", "gy"), P(), P(), P()),
        check_vma=False,
    )
```

profile of v0, /device:TPU:0, one launch (start us, length us, event | category | flops | bytes accessed | tf_op | source)
XLA Modules:
  0.0 642.7 jit_solution(11449475301091532205)
XLA Ops:
  8.0 2.4 collective-permute-start.1
  14.4 5.8 collective-permute-start.25
  24.3 1.9 copy.1395
  30.3 3.4 collective-permute-start.3
  33.7 1.3 collective-permute-start.2
  35.9 5.2 collective-permute-start.27
  44.1 2.1 copy.1387
  46.2 2.5 convolution_tanh_fusion
  50.0 5.2 fusion.164
  58.3 2.8 fusion.175
  64.0 1.7 collective-permute-start.28
  65.7 3.4 collective-permute-start.29
  70.2 4.3 collective-permute-start.31
  75.9 1.7 collective-permute-done.31
  77.6 5.0 collective-permute-done.30
  85.2 3.2 collective-permute-start.5
  92.4 7.0 %collective-permute-start.32 = (bf16[5,1,8,8]{3,2,1,0:T(8,128)(2,1)S(1)}, bf16[5,1,8,8]{3,2,1,0:T(8,128)(2,1)S(1)}, u32[]{:S(2)}, u32[]{:S(2)}) collective-permute-start(bf16[5,1,8,8]{3,2,1,0:T(8,128)(2,1)S(1)} %get-tuple-element.302), channel_id=1, source_target_pairs={{0,8},{8,16},{16,24},{1,9},{9,17},{17,25},{2,10},{10,18},{18,26},{... | collective-permute-start | bytes 1928 | tf_op jit(solution)/shard_map/ppermute | solution.py:21
  101.6 5.4 collective-permute-start.34
  107.7 3.3 collective-permute-start.41
  112.3 1.4 fusion.898
  113.8 4.5 collective-permute-start.7
  118.4 1.3 collective-permute-start.6
  120.1 4.6 collective-permute-start.43
  124.7 1.3 collective-permute-start.42
  126.4 3.9 collective-permute-start.9
  130.3 1.3 collective-permute-start.8
  132.1 1.8 collective-permute-done.8
  133.9 5.4 collective-permute-start.11
  141.6 5.2 collective-permute-done.10
  147.8 3.7 collective-permute-start.13
  153.2 2.0 collective-permute-done.12
  155.3 4.8 collective-permute-start.15
  162.4 4.3 collective-permute-done.14
  168.9 1.9 copy.1400
  170.8 2.5 fusion.691
  174.6 5.2 fusion.162
  181.3 4.2 collective-permute-start.36
  186.6 2.8 fusion.173
  206.7 4.5 collective-permute-start.38
  215.4 3.7 collective-permute-start.44
  232.7 5.0 collective-permute-start.46
  239.0 2.8 fusion.171
  244.2 3.7 collective-permute-start.49
  249.0 4.5 collective-permute-start.51
  254.9 1.7 collective-permute-done.51
  256.6 5.3 collective-permute-done.50
  265.2 3.6 collective-permute-start.53
  269.0 5.0 collective-permute-start.17
  277.2 4.8 collective-permute-start.19
  283.7 5.2 collective-permute-start.55
  291.5 5.4 collective-permute-done.54
  299.9 2.8 collective-permute-start.21
  305.6 4.4 collective-permute-start.56
  319.4 4.5 collective-permute-start.58
  326.7 1.4 fusion.899
  329.5 3.5 collective-permute-start.60
  340.2 4.7 collective-permute-start.62
  371.5 4.9 collective-permute-start.23
  378.1 1.6 collective-permute-done.23
  379.7 5.2 collective-permute-done.22
  386.8 111.3 %all-reduce.6.cloned.1.call-done = (f32[64,135]{0,1:T(8,128)}, f32[5,1728]{1,0:T(8,128)}) async-done(((f32[64,135]{0,1:T(8,128)}, f32[5,1728]{1,0:T(8,128)}), (f32[64,135]{0,1:T(8,128)}, f32[5,1728]{1,0:T(8,128)})) %all-reduce.6.cloned.1.call-update) | async-done | bytes 69136 | tf_op jit(solution)/shard_map/psum | solution.py:266
  498.1 1.6 copy.1540
  499.7 133.0 %all-reduce.4.cloned.1.call-done = f32[64,1728]{0,1:T(8,128)} async-done(((f32[64,1728]{0,1:T(8,128)}), f32[64,1728]{0,1:T(8,128)}) %all-reduce.4.cloned.1.call-update) | async-done | bytes 442384 | tf_op jit(solution)/shard_map/psum | solution.py:266
  632.7 2.2 copy.1541
  (783 shorter events, 158.4 us)
Async XLA Ops:
  7.2 491.0 %all-reduce.6.cloned.1.call-start = ((), (), s32[]{:S(2)}) async-start(), calls=%async_computation.1 | async-start | bytes 253952 | tf_op jit(solution)/shard_map/psum | solution.py:266
  8.0 21.2 %collective-permute-start.1 = (f32[5,3,8,8]{3,2,1,0:T(8,128)S(1)}, f32[5,3,8,8]{3,2,1,0:T(8,128)S(1)}, u32[]{:S(2)}, u32[]{:S(2)}) collective-permute-start(f32[5,3,8,8]{3,2,1,0:T(8,128)S(1)} %get-tuple-element.273), channel_id=1, source_target_pairs={{0,8},{8,16},{16,24},{1,9},{9,17},{17,25},{2,10},{10,18},{18,26},{... | collective-permute-start | bytes 11528 | tf_op jit(solution)/shard_map/ppermute | solution.py:21
  10.5 19.8 %collective-permute-start = (f32[5,3,8,8]{3,2,1,0:T(8,128)S(1)}, f32[5,3,8,8]{3,2,1,0:T(8,128)S(1)}, u32[]{:S(2)}, u32[]{:S(2)}) collective-permute-start(f32[5,3,8,8]{3,2,1,0:T(8,128)S(1)} %get-tuple-element.272), channel_id=1, source_target_pairs={{8,0},{16,8},{24,16},{9,1},{17,9},{25,17},{10,2},{18,10},{26,18},{... | collective-permute-start | bytes 11528 | tf_op jit(solution)/shard_map/ppermute | solution.py:23
  13.1 21.9 %collective-permute-start.24 = (f32[8,3,8,8]{3,2,1,0:T(8,128)S(1)}, f32[8,3,8,8]{3,2,1,0:T(8,128)S(1)}, u32[]{:S(2)}, u32[]{:S(2)}) collective-permute-start(f32[8,3,8,8]{3,2,1,0:T(8,128)S(1)} %get-tuple-element.202), channel_id=1, source_target_pairs={{8,0},{16,8},{24,16},{9,1},{17,9},{25,17},{10,2},{18,10},{26,18},{... | collective-permute-start | bytes 18440 | tf_op jit(solution)/shard_map/ppermute | solution.py:23
  14.4 20.6 %collective-permute-start.25 = (f32[8,3,8,8]{3,2,1,0:T(8,128)S(1)}, f32[8,3,8,8]{3,2,1,0:T(8,128)S(1)}, u32[]{:S(2)}, u32[]{:S(2)}) collective-permute-start(f32[8,3,8,8]{3,2,1,0:T(8,128)S(1)} %get-tuple-element.201), channel_id=1, source_target_pairs={{0,8},{8,16},{16,24},{1,9},{9,17},{17,25},{2,10},{10,18},{18,26},{... | collective-permute-start | bytes 18440 | tf_op jit(solution)/shard_map/ppermute | solution.py:21
  30.3 12.2 %collective-permute-start.3 = (f32[5,10,3,8]{3,2,1,0:T(4,128)S(1)}, f32[5,10,3,8]{3,2,1,0:T(4,128)S(1)}, u32[]{:S(2)}, u32[]{:S(2)}) collective-permute-start(f32[5,10,3,8]{3,2,1,0:T(4,128)S(1)} %get-tuple-element.153), channel_id=1, source_target_pairs={{0,1},{1,2},{2,3},{3,4},{4,5},{5,6},{6,7},{8,9},{9,10},{10,11},{11... | collective-permute-start | bytes 14408 | tf_op jit(solution)/shard_map/ppermute | solution.py:21
  33.7 8.7 %collective-permute-start.2 = (f32[5,10,3,8]{3,2,1,0:T(4,128)S(1)}, f32[5,10,3,8]{3,2,1,0:T(4,128)S(1)}, u32[]{:S(2)}, u32[]{:S(2)}) collective-permute-start(f32[5,10,3,8]{3,2,1,0:T(4,128)S(1)} %get-tuple-element.152), channel_id=1, source_target_pairs={{1,0},{2,1},{3,2},{4,3},{5,4},{6,5},{7,6},{9,8},{10,9},{11,10},{12... | collective-permute-start | bytes 14408 | tf_op jit(solution)/shard_map/ppermute | solution.py:23
  35.9 27.0 %collective-permute-start.27 = (f32[8,10,3,8]{3,2,1,0:T(4,128)}, f32[8,10,3,8]{3,2,1,0:T(4,128)}, u32[]{:S(2)}, u32[]{:S(2)}) collective-permute-start(f32[8,10,3,8]{3,2,1,0:T(4,128)} %get-tuple-element.95), channel_id=1, source_target_pairs={{0,1},{1,2},{2,3},{3,4},{4,5},{5,6},{6,7},{8,9},{9,10},{10,11},{11... | collective-permute-start | bytes 23048 | tf_op jit(solution)/shard_map/ppermute | solution.py:21
  41.1 21.8 %collective-permute-start.26 = (f32[8,10,3,8]{3,2,1,0:T(4,128)}, f32[8,10,3,8]{3,2,1,0:T(4,128)}, u32[]{:S(2)}, u32[]{:S(2)}) collective-permute-start(f32[8,10,3,8]{3,2,1,0:T(4,128)} %get-tuple-element.94), channel_id=1, source_target_pairs={{1,0},{2,1},{3,2},{4,3},{5,4},{6,5},{7,6},{9,8},{10,9},{11,10},{12... | collective-permute-start | bytes 23048 | tf_op jit(solution)/shard_map/ppermute | solution.py:23
  64.0 5.4 collective-permute-start.28
  65.7 4.4 collective-permute-start.29
  70.2 7.4 %collective-permute-start.31 = (f32[8,10,3,8]{3,2,1,0:T(4,128)S(1)}, f32[8,10,3,8]{3,2,1,0:T(4,128)S(1)}, u32[]{:S(2)}, u32[]{:S(2)}) collective-permute-start(f32[8,10,3,8]{3,2,1,0:T(4,128)S(1)} %get-tuple-element.93), channel_id=1, source_target_pairs={{0,1},{1,2},{2,3},{3,4},{4,5},{5,6},{6,7},{8,9},{9,10},{10,11},{11... | collective-permute-start | bytes 23048 | tf_op jit(solution)/shard_map/ppermute | solution.py:21
  74.5 8.1 %collective-permute-start.30 = (f32[8,10,3,8]{3,2,1,0:T(4,128)S(1)}, f32[8,10,3,8]{3,2,1,0:T(4,128)S(1)}, u32[]{:S(2)}, u32[]{:S(2)}) collective-permute-start(f32[8,10,3,8]{3,2,1,0:T(4,128)S(1)} %get-tuple-element.92), channel_id=1, source_target_pairs={{1,0},{2,1},{3,2},{4,3},{5,4},{6,5},{7,6},{9,8},{10,9},{11,10},{12... | collective-permute-start | bytes 23048 | tf_op jit(solution)/shard_map/ppermute | solution.py:23
  85.2 28.6 %collective-permute-start.5 = (f32[5,3,8,8]{3,2,1,0:T(8,128)S(1)}, f32[5,3,8,8]{3,2,1,0:T(8,128)S(1)}, u32[]{:S(2)}, u32[]{:S(2)}) collective-permute-start(f32[5,3,8,8]{3,2,1,0:T(8,128)S(1)} %get-tuple-element.264), channel_id=1, source_target_pairs={{0,8},{8,16},{16,24},{1,9},{9,17},{17,25},{2,10},{10,18},{18,26},{... | collective-permute-start | bytes 11528 | tf_op jit(solution)/shard_map/ppermute | solution.py:21
  88.4 25.4 %collective-permute-start.4 = (f32[5,3,8,8]{3,2,1,0:T(8,128)S(1)}, f32[5,3,8,8]{3,2,1,0:T(8,128)S(1)}, u32[]{:S(2)}, u32[]{:S(2)}) collective-permute-start(f32[5,3,8,8]{3,2,1,0:T(8,128)S(1)} %get-tuple-element.265), channel_id=1, source_target_pairs={{8,0},{16,8},{24,16},{9,1},{17,9},{25,17},{10,2},{18,10},{26,18},{... | collective-permute-start | bytes 11528 | tf_op jit(solution)/shard_map/ppermute | solution.py:23
  89.7 30.3 %collective-permute-start.40 = (f32[8,3,8,8]{3,2,1,0:T(8,128)S(1)}, f32[8,3,8,8]{3,2,1,0:T(8,128)S(1)}, u32[]{:S(2)}, u32[]{:S(2)}) collective-permute-start(f32[8,3,8,8]{3,2,1,0:T(8,128)S(1)} %get-tuple-element.192), channel_id=1, source_target_pairs={{8,0},{16,8},{24,16},{9,1},{17,9},{25,17},{10,2},{18,10},{26,18},{... | collective-permute-start | bytes 18440 | tf_op jit(solution)/shard_map/ppermute | solution.py:23
  91.1 8.9 %collective-permute-start.33 = (bf16[5,1,8,8]{3,2,1,0:T(8,128)(2,1)S(1)}, bf16[5,1,8,8]{3,2,1,0:T(8,128)(2,1)S(1)}, u32[]{:S(2)}, u32[]{:S(2)}) collective-permute-start(bf16[5,1,8,8]{3,2,1,0:T(8,128)(2,1)S(1)} %get-tuple-element.303), channel_id=1, source_target_pairs={{8,0},{16,8},{24,16},{9,1},{17,9},{25,17},{10,2},{18,10},{26,18},{... | collective-permute-start | bytes 1928 | tf_op jit(solution)/shard_map/ppermute | solution.py:23
  92.4 7.9 %collective-permute-start.32 = (bf16[5,1,8,8]{3,2,1,0:T(8,128)(2,1)S(1)}, bf16[5,1,8,8]{3,2,1,0:T(8,128)(2,1)S(1)}, u32[]{:S(2)}, u32[]{:S(2)}) collective-permute-start(bf16[5,1,8,8]{3,2,1,0:T(8,128)(2,1)S(1)} %get-tuple-element.302), channel_id=1, source_target_pairs={{0,8},{8,16},{16,24},{1,9},{9,17},{17,25},{2,10},{10,18},{18,26},{... | collective-permute-start | bytes 1928 | tf_op jit(solution)/shard_map/ppermute | solution.py:21
  100.3 6.8 %collective-permute-start.35 = (bf16[5,6,1,8]{3,2,1,0:T(2,128)(2,1)S(1)}, bf16[5,6,1,8]{3,2,1,0:T(2,128)(2,1)S(1)}, u32[]{:S(2)}, u32[]{:S(2)}) collective-permute-start(bf16[5,6,1,8]{3,2,1,0:T(2,128)(2,1)S(1)} %get-tuple-element.285), channel_id=1, source_target_pairs={{1,0},{2,1},{3,2},{4,3},{5,4},{6,5},{7,6},{9,8},{10,9},{11,10},{12... | collective-permute-start | bytes 1448 | tf_op jit(solution)/shard_map/ppermute | solution.py:23
  101.6 9.4 %collective-permute-start.34 = (bf16[5,6,1,8]{3,2,1,0:T(2,128)(2,1)S(1)}, bf16[5,6,1,8]{3,2,1,0:T(2,128)(2,1)S(1)}, u32[]{:S(2)}, u32[]{:S(2)}) collective-permute-start(bf16[5,6,1,8]{3,2,1,0:T(2,128)(2,1)S(1)} %get-tuple-element.284), channel_id=1, source_target_pairs={{0,1},{1,2},{2,3},{3,4},{4,5},{5,6},{6,7},{8,9},{9,10},{10,11},{11... | collective-permute-start | bytes 1448 | tf_op jit(solution)/shard_map/ppermute | solution.py:21
  107.7 12.3 %collective-permute-start.41 = (f32[8,3,8,8]{3,2,1,0:T(8,128)S(1)}, f32[8,3,8,8]{3,2,1,0:T(8,128)S(1)}, u32[]{:S(2)}, u32[]{:S(2)}) collective-permute-start(f32[8,3,8,8]{3,2,1,0:T(8,128)S(1)} %get-tuple-element.191), channel_id=1, source_target_pairs={{0,8},{8,16},{16,24},{1,9},{9,17},{17,25},{2,10},{10,18},{18,26},{... | collective-permute-start | bytes 18440 | tf_op jit(solution)/shard_map/ppermute | solution.py:21
  113.8 12.2 %collective-permute-start.7 = (f32[5,10,3,8]{3,2,1,0:T(4,128)S(1)}, f32[5,10,3,8]{3,2,1,0:T(4,128)S(1)}, u32[]{:S(2)}, u32[]{:S(2)}) collective-permute-start(f32[5,10,3,8]{3,2,1,0:T(4,128)S(1)} %get-tuple-element.149), channel_id=1, source_target_pairs={{0,1},{1,2},{2,3},{3,4},{4,5},{5,6},{6,7},{8,9},{9,10},{10,11},{11... | collective-permute-start | bytes 14408 | tf_op jit(solution)/shard_map/ppermute | solution.py:21
  118.4 7.7 %collective-permute-start.6 = (f32[5,10,3,8]{3,2,1,0:T(4,128)S(1)}, f32[5,10,3,8]{3,2,1,0:T(4,128)S(1)}, u32[]{:S(2)}, u32[]{:S(2)}) collective-permute-start(f32[5,10,3,8]{3,2,1,0:T(4,128)S(1)} %get-tuple-element.148), channel_id=1, source_target_pairs={{1,0},{2,1},{3,2},{4,3},{5,4},{6,5},{7,6},{9,8},{10,9},{11,10},{12... | collective-permute-start | bytes 14408 | tf_op jit(solution)/shard_map/ppermute | solution.py:23
  120.1 20.9 %collective-permute-start.43 = (f32[8,10,3,8]{3,2,1,0:T(4,128)S(1)}, f32[8,10,3,8]{3,2,1,0:T(4,128)S(1)}, u32[]{:S(2)}, u32[]{:S(2)}) collective-permute-start(f32[8,10,3,8]{3,2,1,0:T(4,128)S(1)} %get-tuple-element.91), channel_id=1, source_target_pairs={{0,1},{1,2},{2,3},{3,4},{4,5},{5,6},{6,7},{8,9},{9,10},{10,11},{11... | collective-permute-start | bytes 23048 | tf_op jit(solution)/shard_map/ppermute | solution.py:21
  124.7 16.3 %collective-permute-start.42 = (f32[8,10,3,8]{3,2,1,0:T(4,128)S(1)}, f32[8,10,3,8]{3,2,1,0:T(4,128)S(1)}, u32[]{:S(2)}, u32[]{:S(2)}) collective-permute-start(f32[8,10,3,8]{3,2,1,0:T(4,128)S(1)} %get-tuple-element.90), channel_id=1, source_target_pairs={{1,0},{2,1},{3,2},{4,3},{5,4},{6,5},{7,6},{9,8},{10,9},{11,10},{12... | collective-permute-start | bytes 23048 | tf_op jit(solution)/shard_map/ppermute | solution.py:23
  126.4 5.7 collective-permute-start.9
  133.9 7.7 %collective-permute-start.11 = (f32[5,10,3,8]{3,2,1,0:T(4,128)S(1)}, f32[5,10,3,8]{3,2,1,0:T(4,128)S(1)}, u32[]{:S(2)}, u32[]{:S(2)}) collective-permute-start(f32[5,10,3,8]{3,2,1,0:T(4,128)S(1)} %get-tuple-element.147), channel_id=1, source_target_pairs={{0,1},{1,2},{2,3},{3,4},{4,5},{5,6},{6,7},{8,9},{9,10},{10,11},{11... | collective-permute-start | bytes 14408 | tf_op jit(solution)/shard_map/ppermute | solution.py:21
  139.4 7.5 %collective-permute-start.10 = (f32[5,10,3,8]{3,2,1,0:T(4,128)S(1)}, f32[5,10,3,8]{3,2,1,0:T(4,128)S(1)}, u32[]{:S(2)}, u32[]{:S(2)}) collective-permute-start(f32[5,10,3,8]{3,2,1,0:T(4,128)S(1)} %get-tuple-element.146), channel_id=1, source_target_pairs={{1,0},{2,1},{3,2},{4,3},{5,4},{6,5},{7,6},{9,8},{10,9},{11,10},{12... | collective-permute-start | bytes 14408 | tf_op jit(solution)/shard_map/ppermute | solution.py:23
  147.8 5.4 collective-permute-start.13
  151.4 3.8 collective-permute-start.12
  155.3 11.4 %collective-permute-start.15 = (f32[5,10,3,8]{3,2,1,0:T(4,128)S(1)}, f32[5,10,3,8]{3,2,1,0:T(4,128)S(1)}, u32[]{:S(2)}, u32[]{:S(2)}) collective-permute-start(f32[5,10,3,8]{3,2,1,0:T(4,128)S(1)} %get-tuple-element.145), channel_id=1, source_target_pairs={{0,1},{1,2},{2,3},{3,4},{4,5},{5,6},{6,7},{8,9},{9,10},{10,11},{11... | collective-permute-start | bytes 14408 | tf_op jit(solution)/shard_map/ppermute | solution.py:21
  160.1 6.6 %collective-permute-start.14 = (f32[5,10,3,8]{3,2,1,0:T(4,128)S(1)}, f32[5,10,3,8]{3,2,1,0:T(4,128)S(1)}, u32[]{:S(2)}, u32[]{:S(2)}) collective-permute-start(f32[5,10,3,8]{3,2,1,0:T(4,128)S(1)} %get-tuple-element.144), channel_id=1, source_target_pairs={{1,0},{2,1},{3,2},{4,3},{5,4},{6,5},{7,6},{9,8},{10,9},{11,10},{12... | collective-permute-start | bytes 14408 | tf_op jit(solution)/shard_map/ppermute | solution.py:23
  180.0 24.7 %collective-permute-start.37 = (bf16[64,1,8,8]{0,3,2,1:T(8,128)(2,1)S(1)}, bf16[64,1,8,8]{0,3,2,1:T(8,128)(2,1)S(1)}, u32[]{:S(2)}, u32[]{:S(2)}) collective-permute-start(bf16[64,1,8,8]{0,3,2,1:T(8,128)(2,1)S(1)} %get-tuple-element.281), channel_id=1, source_target_pairs={{8,0},{16,8},{24,16},{9,1},{17,9},{25,17},{10,2},{18,10},{26,18},{... | collective-permute-start | bytes 24584 | tf_op jit(solution)/shard_map/ppermute | solution.py:23
  181.3 23.4 %collective-permute-start.36 = (bf16[64,1,8,8]{0,3,2,1:T(8,128)(2,1)S(1)}, bf16[64,1,8,8]{0,3,2,1:T(8,128)(2,1)S(1)}, u32[]{:S(2)}, u32[]{:S(2)}) collective-permute-start(bf16[64,1,8,8]{0,3,2,1:T(8,128)(2,1)S(1)} %get-tuple-element.280), channel_id=1, source_target_pairs={{0,8},{8,16},{16,24},{1,9},{9,17},{17,25},{2,10},{10,18},{18,26},{... | collective-permute-start | bytes 24584 | tf_op jit(solution)/shard_map/ppermute | solution.py:21
  205.4 7.6 %collective-permute-start.39 = (bf16[64,6,1,8]{0,3,2,1:T(8,128)(2,1)S(1)}, bf16[64,6,1,8]{0,3,2,1:T(8,128)(2,1)S(1)}, u32[]{:S(2)}, u32[]{:S(2)}) collective-permute-start(bf16[64,6,1,8]{0,3,2,1:T(8,128)(2,1)S(1)} %get-tuple-element.228), channel_id=1, source_target_pairs={{1,0},{2,1},{3,2},{4,3},{5,4},{6,5},{7,6},{9,8},{10,9},{11,10},{12... | collective-permute-start | bytes 18440 | tf_op jit(solution)/shard_map/ppermute | solution.py:23
  206.7 6.3 collective-permute-start.38
  214.1 17.3 %collective-permute-start.45 = (bf16[64,1,8,8]{0,3,2,1:T(8,128)(2,1)S(1)}, bf16[64,1,8,8]{0,3,2,1:T(8,128)(2,1)S(1)}, u32[]{:S(2)}, u32[]{:S(2)}) collective-permute-start(bf16[64,1,8,8]{0,3,2,1:T(8,128)(2,1)S(1)} %get-tuple-element.279), channel_id=1, source_target_pairs={{8,0},{16,8},{24,16},{9,1},{17,9},{25,17},{10,2},{18,10},{26,18},{... | collective-permute-start | bytes 24584 | tf_op jit(solution)/shard_map/ppermute | solution.py:23
  215.4 16.0 %collective-permute-start.44 = (bf16[64,1,8,8]{0,3,2,1:T(8,128)(2,1)S(1)}, bf16[64,1,8,8]{0,3,2,1:T(8,128)(2,1)S(1)}, u32[]{:S(2)}, u32[]{:S(2)}) collective-permute-start(bf16[64,1,8,8]{0,3,2,1:T(8,128)(2,1)S(1)} %get-tuple-element.278), channel_id=1, source_target_pairs={{0,8},{8,16},{16,24},{1,9},{9,17},{17,25},{2,10},{10,18},{18,26},{... | collective-permute-start | bytes 24584 | tf_op jit(solution)/shard_map/ppermute | solution.py:21
  231.4 6.5 %collective-permute-start.47 = (bf16[64,6,1,8]{0,3,2,1:T(8,128)(2,1)S(1)}, bf16[64,6,1,8]{0,3,2,1:T(8,128)(2,1)S(1)}, u32[]{:S(2)}, u32[]{:S(2)}) collective-permute-start(bf16[64,6,1,8]{0,3,2,1:T(8,128)(2,1)S(1)} %get-tuple-element.226), channel_id=1, source_target_pairs={{1,0},{2,1},{3,2},{4,3},{5,4},{6,5},{7,6},{9,8},{10,9},{11,10},{12... | collective-permute-start | bytes 18440 | tf_op jit(solution)/shard_map/ppermute | solution.py:23
  232.7 6.1 collective-permute-start.46
  242.9 5.3 collective-permute-start.48
  244.2 4.7 collective-permute-start.49
  249.0 7.7 %collective-permute-start.51 = (f32[8,10,3,8]{3,2,1,0:T(4,128)S(1)}, f32[8,10,3,8]{3,2,1,0:T(4,128)S(1)}, u32[]{:S(2)}, u32[]{:S(2)}) collective-permute-start(f32[8,10,3,8]{3,2,1,0:T(4,128)S(1)} %get-tuple-element.89), channel_id=1, source_target_pairs={{0,1},{1,2},{2,3},{3,4},{4,5},{5,6},{6,7},{8,9},{9,10},{10,11},{11... | collective-permute-start | bytes 23048 | tf_op jit(solution)/shard_map/ppermute | solution.py:21
  253.5 8.4 %collective-permute-start.50 = (f32[8,10,3,8]{3,2,1,0:T(4,128)S(1)}, f32[8,10,3,8]{3,2,1,0:T(4,128)S(1)}, u32[]{:S(2)}, u32[]{:S(2)}) collective-permute-start(f32[8,10,3,8]{3,2,1,0:T(4,128)S(1)} %get-tuple-element.88), channel_id=1, source_target_pairs={{1,0},{2,1},{3,2},{4,3},{5,4},{6,5},{7,6},{9,8},{10,9},{11,10},{12... | collective-permute-start | bytes 23048 | tf_op jit(solution)/shard_map/ppermute | solution.py:23
  263.9 19.7 %collective-permute-start.52 = (f32[8,3,8,8]{3,2,1,0:T(8,128)S(1)}, f32[8,3,8,8]{3,2,1,0:T(8,128)S(1)}, u32[]{:S(2)}, u32[]{:S(2)}) collective-permute-start(f32[8,3,8,8]{3,2,1,0:T(8,128)S(1)} %get-tuple-element.182), channel_id=1, source_target_pairs={{8,0},{16,8},{24,16},{9,1},{17,9},{25,17},{10,2},{18,10},{26,18},{... | collective-permute-start | bytes 18440 | tf_op jit(solution)/shard_map/ppermute | solution.py:23
  265.2 18.4 %collective-permute-start.53 = (f32[8,3,8,8]{3,2,1,0:T(8,128)S(1)}, f32[8,3,8,8]{3,2,1,0:T(8,128)S(1)}, u32[]{:S(2)}, u32[]{:S(2)}) collective-permute-start(f32[8,3,8,8]{3,2,1,0:T(8,128)S(1)} %get-tuple-element.181), channel_id=1, source_target_pairs={{0,8},{8,16},{16,24},{1,9},{9,17},{17,25},{2,10},{10,18},{18,26},{... | collective-permute-start | bytes 18440 | tf_op jit(solution)/shard_map/ppermute | solution.py:21
  269.0 6.9 %collective-permute-start.17 = (f32[5,3,8,8]{3,2,1,0:T(8,128)S(1)}, f32[5,3,8,8]{3,2,1,0:T(8,128)S(1)}, u32[]{:S(2)}, u32[]{:S(2)}) collective-permute-start(f32[5,3,8,8]{3,2,1,0:T(8,128)S(1)} %get-tuple-element.246), channel_id=1, source_target_pairs={{0,8},{8,16},{16,24},{1,9},{9,17},{17,25},{2,10},{10,18},{18,26},{... | collective-permute-start | bytes 11528 | tf_op jit(solution)/shard_map/ppermute | solution.py:21
  277.2 13.1 %collective-permute-start.19 = (f32[5,10,3,8]{3,2,1,0:T(4,128)S(1)}, f32[5,10,3,8]{3,2,1,0:T(4,128)S(1)}, u32[]{:S(2)}, u32[]{:S(2)}) collective-permute-start(f32[5,10,3,8]{3,2,1,0:T(4,128)S(1)} %get-tuple-element.141), channel_id=1, source_target_pairs={{0,1},{1,2},{2,3},{3,4},{4,5},{5,6},{6,7},{8,9},{9,10},{10,11},{11... | collective-permute-start | bytes 14408 | tf_op jit(solution)/shard_map/ppermute | solution.py:21
  282.0 8.3 %collective-permute-start.18 = (f32[5,10,3,8]{3,2,1,0:T(4,128)S(1)}, f32[5,10,3,8]{3,2,1,0:T(4,128)S(1)}, u32[]{:S(2)}, u32[]{:S(2)}) collective-permute-start(f32[5,10,3,8]{3,2,1,0:T(4,128)S(1)} %get-tuple-element.140), channel_id=1, source_target_pairs={{1,0},{2,1},{3,2},{4,3},{5,4},{6,5},{7,6},{9,8},{10,9},{11,10},{12... | collective-permute-start | bytes 14408 | tf_op jit(solution)/shard_map/ppermute | solution.py:23
  283.7 7.8 %collective-permute-start.55 = (f32[8,10,3,8]{3,2,1,0:T(4,128)S(1)}, f32[8,10,3,8]{3,2,1,0:T(4,128)}, u32[]{:S(2)}, u32[]{:S(2)}) collective-permute-start(f32[8,10,3,8]{3,2,1,0:T(4,128)S(1)} %get-tuple-element.87), channel_id=1, source_target_pairs={{0,1},{1,2},{2,3},{3,4},{4,5},{5,6},{6,7},{8,9},{9,10},{10,11},{11... | collective-permute-start | bytes 23048 | tf_op jit(solution)/shard_map/ppermute | solution.py:21
  288.9 8.0 %collective-permute-start.54 = (f32[8,10,3,8]{3,2,1,0:T(4,128)S(1)}, f32[8,10,3,8]{3,2,1,0:T(4,128)}, u32[]{:S(2)}, u32[]{:S(2)}) collective-permute-start(f32[8,10,3,8]{3,2,1,0:T(4,128)S(1)} %get-tuple-element.86), channel_id=1, source_target_pairs={{1,0},{2,1},{3,2},{4,3},{5,4},{6,5},{7,6},{9,8},{10,9},{11,10},{12... | collective-permute-start | bytes 23048 | tf_op jit(solution)/shard_map/ppermute | solution.py:23
  299.9 71.5 %collective-permute-start.21 = (f32[5,3,8,8]{3,2,1,0:T(8,128)}, f32[5,3,8,8]{3,2,1,0:T(8,128)S(1)}, u32[]{:S(2)}, u32[]{:S(2)}) collective-permute-start(f32[5,3,8,8]{3,2,1,0:T(8,128)} %get-tuple-element.243), channel_id=1, source_target_pairs={{0,8},{8,16},{16,24},{1,9},{9,17},{17,25},{2,10},{10,18},{18,26},{... | collective-permute-start | bytes 11528 | tf_op jit(solution)/shard_map/ppermute | solution.py:21
  302.7 68.7 %collective-permute-start.20 = (f32[5,3,8,8]{3,2,1,0:T(8,128)}, f32[5,3,8,8]{3,2,1,0:T(8,128)S(1)}, u32[]{:S(2)}, u32[]{:S(2)}) collective-permute-start(f32[5,3,8,8]{3,2,1,0:T(8,128)} %get-tuple-element.242), channel_id=1, source_target_pairs={{8,0},{16,8},{24,16},{9,1},{17,9},{25,17},{10,2},{18,10},{26,18},{... | collective-permute-start | bytes 11528 | tf_op jit(solution)/shard_map/ppermute | solution.py:23
  304.3 13.8 %collective-permute-start.57 = (bf16[5,1,8,8]{3,2,1,0:T(8,128)(2,1)S(1)}, bf16[5,1,8,8]{3,2,1,0:T(8,128)(2,1)S(1)}, u32[]{:S(2)}, u32[]{:S(2)}) collective-permute-start(bf16[5,1,8,8]{3,2,1,0:T(8,128)(2,1)S(1)} %get-tuple-element.301), channel_id=1, source_target_pairs={{8,0},{16,8},{24,16},{9,1},{17,9},{25,17},{10,2},{18,10},{26,18},{... | collective-permute-start | bytes 1928 | tf_op jit(solution)/shard_map/ppermute | solution.py:23
  305.6 12.5 %collective-permute-start.56 = (bf16[5,1,8,8]{3,2,1,0:T(8,128)(2,1)S(1)}, bf16[5,1,8,8]{3,2,1,0:T(8,128)(2,1)S(1)}, u32[]{:S(2)}, u32[]{:S(2)}) collective-permute-start(bf16[5,1,8,8]{3,2,1,0:T(8,128)(2,1)S(1)} %get-tuple-element.300), channel_id=1, source_target_pairs={{0,8},{8,16},{16,24},{1,9},{9,17},{17,25},{2,10},{10,18},{18,26},{... | collective-permute-start | bytes 1928 | tf_op jit(solution)/shard_map/ppermute | solution.py:21
  318.1 6.8 %collective-permute-start.59 = (bf16[5,6,1,8]{3,2,1,0:T(2,128)(2,1)S(1)}, bf16[5,6,1,8]{3,2,1,0:T(2,128)(2,1)S(1)}, u32[]{:S(2)}, u32[]{:S(2)}) collective-permute-start(bf16[5,6,1,8]{3,2,1,0:T(2,128)(2,1)S(1)} %get-tuple-element.283), channel_id=1, source_target_pairs={{1,0},{2,1},{3,2},{4,3},{5,4},{6,5},{7,6},{9,8},{10,9},{11,10},{12... | collective-permute-start | bytes 1448 | tf_op jit(solution)/shard_map/ppermute | solution.py:23
  319.4 6.0 collective-permute-start.58
  328.2 10.7 %collective-permute-start.61 = (bf16[64,1,8,8]{0,3,2,1:T(8,128)(2,1)S(1)}, bf16[64,1,8,8]{0,3,2,1:T(8,128)(2,1)S(1)}, u32[]{:S(2)}, u32[]{:S(2)}) collective-permute-start(bf16[64,1,8,8]{0,3,2,1:T(8,128)(2,1)S(1)} %get-tuple-element.277), channel_id=1, source_target_pairs={{8,0},{16,8},{24,16},{9,1},{17,9},{25,17},{10,2},{18,10},{26,18},{... | collective-permute-start | bytes 24584 | tf_op jit(solution)/shard_map/ppermute | solution.py:23
  329.5 9.4 %collective-permute-start.60 = (bf16[64,1,8,8]{0,3,2,1:T(8,128)(2,1)S(1)}, bf16[64,1,8,8]{0,3,2,1:T(8,128)(2,1)S(1)}, u32[]{:S(2)}, u32[]{:S(2)}) collective-permute-start(bf16[64,1,8,8]{0,3,2,1:T(8,128)(2,1)S(1)} %get-tuple-element.276), channel_id=1, source_target_pairs={{0,8},{8,16},{16,24},{1,9},{9,17},{17,25},{2,10},{10,18},{18,26},{... | collective-permute-start | bytes 24584 | tf_op jit(solution)/shard_map/ppermute | solution.py:21
  338.9 6.2 collective-permute-start.63
  340.2 6.1 collective-permute-start.62
  369.3 263.5 %all-reduce.4.cloned.1.call-start = ((), (), s32[]{:S(2)}) async-start(), calls=%async_computation | async-start | bytes 1769472 | tf_op jit(solution)/shard_map/psum | solution.py:266
  371.5 8.2 %collective-permute-start.23 = (f32[5,10,3,8]{3,2,1,0:T(4,128)S(1)}, f32[5,10,3,8]{3,2,1,0:T(4,128)S(1)}, u32[]{:S(2)}, u32[]{:S(2)}) collective-permute-start(f32[5,10,3,8]{3,2,1,0:T(4,128)S(1)} %get-tuple-element.139), channel_id=1, source_target_pairs={{0,1},{1,2},{2,3},{3,4},{4,5},{5,6},{6,7},{8,9},{9,10},{10,11},{11... | collective-permute-start | bytes 14408 | tf_op jit(solution)/shard_map/ppermute | solution.py:21
  376.5 8.5 %collective-permute-start.22 = (f32[5,10,3,8]{3,2,1,0:T(4,128)S(1)}, f32[5,10,3,8]{3,2,1,0:T(4,128)S(1)}, u32[]{:S(2)}, u32[]{:S(2)}) collective-permute-start(f32[5,10,3,8]{3,2,1,0:T(4,128)S(1)} %get-tuple-element.138), channel_id=1, source_target_pairs={{1,0},{2,1},{3,2},{4,3},{5,4},{6,5},{7,6},{9,8},{10,9},{11,10},{12... | collective-permute-start | bytes 14408 | tf_op jit(solution)/shard_map/ppermute | solution.py:23
  (108 other events, 347.3 us)
Sparse Core Ops, SparseCore 0:
  369.4 128.6 all-reduce.5
  503.3 129.3 all-reduce.3
where the time goes:
time: 652 us; the launch traced here: 643 us
  waiting for transfers between devices  289 us (44%)
  starting transfers between devices  182 us (28%)
  local copies, waits for them, and re-layouts  68.4 us (10%)
  matrix products  65.6 us (10%)
  other arithmetic  20.1 us (3%)
  between operations  17.5 us (3%)
    psum x2, waiting for transfers between devices, body(): result = lax.psum((totals[0], totals[1], totals[2]), ('gx', 'gy'))  244 us
    ppermute x32, starting transfers between devices, padded_2(): lax.ppermute(tail, axis, [(i, (i + 1) % count) for i in range(ends)])  140 us
    ppermute x32, starting transfers between devices, padded_2(): lax.ppermute(head, axis, [((i + 1) % count, i) for i in range(ends)])  41.7 us
    unnamed x240, local copies, waits for them, and re-layouts  40.9 us
    dot_general x162, matrix products, kernel_grad(): lax.dot_general(flat_grad, window.reshape(channels, -1), (((1,), (1,)), (...  37 us
    ppermute x32, waiting for transfers between devices, padded_2(): lax.ppermute(head, axis, [((i + 1) % count, i) for i in range(ends)])  35.6 us
    conv_general_dilated x11, matrix products, conv_valid(): lax.conv_general_dilated(padded[None], kernel, (1, 1, 1), 'VALID', dimens...  28.6 us
  transfers between devices with their start and end apart: 66, of which 22 were waited for; matrix products, arithmetic and copies ran while one was open for 14% of the time, Pallas kernels for 0%

commit v1 on v0

--- a/solution.py
+++ b/solution.py
@@ -263,7 +263,7 @@
         )
         if step_index > 0:
             adjoint_in = carried + state_grad
-    result = lax.psum((totals[0], totals[1], totals[2]), ("gx", "gy"))
+    result = lax.psum(lax.psum((totals[0], totals[1], totals[2]), "gx"), "gy")
     return (current.reshape(channels, size_x, size_y * NZ), result[0], result[1], result[2])
 
 

time: 652 us -> 616 us (0.945)
  waiting for transfers between devices: 289 us -> 253 us
    psum x2 -> x4, waiting for transfers between devices: 244 us -> 208 us  [body(): result = lax.psum(lax.psum((totals[0], totals[1], totals[2]), 'gx'), 'gy')]
  transfers between devices with their start and end apart: 66 -> 68, of which waited for: 22 -> 24; matrix products, arithmetic and copies ran while one was open for 14% -> 15% of each run, Pallas kernels for 0% -> 0%
where the time goes in v1:
time: 616 us; the launch traced here: 606 us
  waiting for transfers between devices  253 us (41%)
  starting transfers between devices  182 us (30%)
  local copies, waits for them, and re-layouts  68.5 us (11%)
  matrix products  65.6 us (11%)
  other arithmetic  20.1 us (3%)
  between operations  17.2 us (3%)
    psum x4, waiting for transfers between devices, body(): result = lax.psum(lax.psum((totals[0], totals[1], totals[2]), 'gx'), 'gy')  208 us
    ppermute x32, starting transfers between devices, padded_2(): lax.ppermute(tail, axis, [(i, (i + 1) % count) for i in range(ends)])  140 us
    ppermute x32, starting transfers between devices, padded_2(): lax.ppermute(head, axis, [((i + 1) % count, i) for i in range(ends)])  41.7 us
    unnamed x240, local copies, waits for them, and re-layouts  41 us
    dot_general x162, matrix products, kernel_grad(): lax.dot_general(flat_grad, window.reshape(channels, -1), (((1,), (1,)), (...  37 us
    ppermute x32, waiting for transfers between devices, padded_2(): lax.ppermute(head, axis, [((i + 1) % count, i) for i in range(ends)])  35.6 us
    conv_general_dilated x11, matrix products, conv_valid(): lax.conv_general_dilated(padded[None], kernel, (1, 1, 1), 'VALID', dimens...  28.6 us
  transfers between devices with their start and end apart: 68, of which 24 were waited for; matrix products, arithmetic and copies ran while one was open for 15% of the time, Pallas kernels for 0%

profile of v1, /device:TPU:0, one launch (start us, length us, event | category | flops | bytes accessed | tf_op | source)
XLA Modules:
  0.0 606.3 jit_solution(10952548684228454874)
XLA Ops:
  8.0 2.4 collective-permute-start.1
  14.4 5.8 collective-permute-start.25
  24.3 1.9 copy.1395
  30.3 3.4 collective-permute-start.3
  33.7 1.3 collective-permute-start.2
  35.9 5.2 collective-permute-start.27
  44.1 2.1 copy.1387
  46.2 2.5 convolution_tanh_fusion
  49.9 5.2 fusion.164
  58.3 2.8 fusion.175
  64.0 1.7 collective-permute-start.28
  65.7 3.4 collective-permute-start.29
  70.2 4.3 collective-permute-start.31
  75.9 1.7 collective-permute-done.31
  77.6 5.0 collective-permute-done.30
  85.1 3.2 collective-permute-start.5
  88.4 1.3 collective-permute-start.4
  92.4 7.0 %collective-permute-start.32 = (bf16[5,1,8,8]{3,2,1,0:T(8,128)(2,1)S(1)}, bf16[5,1,8,8]{3,2,1,0:T(8,128)(2,1)S(1)}, u32[]{:S(2)}, u32[]{:S(2)}) collective-permute-start(bf16[5,1,8,8]{3,2,1,0:T(8,128)(2,1)S(1)} %get-tuple-element.304), channel_id=1, source_target_pairs={{0,8},{8,16},{16,24},{1,9},{9,17},{17,25},{2,10},{10,18},{18,26},{... | collective-permute-start | bytes 1928 | tf_op jit(solution)/shard_map/ppermute | solution.py:21
  101.6 5.4 collective-permute-start.34
  107.7 3.3 collective-permute-start.41
  112.3 1.4 fusion.898
  113.8 4.5 collective-permute-start.7
  120.1 4.6 collective-permute-start.43
  126.4 3.9 collective-permute-start.9
  132.1 1.8 collective-permute-done.8
  133.9 5.4 collective-permute-start.11
  141.6 5.2 collective-permute-done.10
  147.8 3.7 collective-permute-start.13
  153.2 2.0 collective-permute-done.12
  155.3 4.8 collective-permute-start.15
  162.4 4.3 collective-permute-done.14
  168.9 1.9 copy.1400
  170.8 2.5 fusion.691
  174.6 5.2 fusion.162
  181.3 4.2 collective-permute-start.36
  186.6 2.8 fusion.173
  206.7 4.5 collective-permute-start.38
  215.4 3.7 collective-permute-start.44
  232.7 5.0 collective-permute-start.46
  239.0 2.8 fusion.171
  244.2 3.7 collective-permute-start.49
  249.0 4.5 collective-permute-start.51
  254.9 1.7 collective-permute-done.51
  256.6 5.3 collective-permute-done.50
  265.2 3.6 collective-permute-start.53
  269.0 5.0 collective-permute-start.17
  277.1 4.8 collective-permute-start.19
  283.7 5.2 collective-permute-start.55
  291.5 5.4 collective-permute-done.54
  299.9 2.8 collective-permute-start.21
  305.6 4.4 collective-permute-start.56
  319.4 4.5 collective-permute-start.58
  326.7 1.4 fusion.899
  329.4 3.5 collective-permute-start.60
  340.2 4.7 collective-permute-start.62
  371.6 4.9 collective-permute-start.23
  378.1 1.6 collective-permute-done.23
  379.6 5.3 collective-permute-done.22
  385.5 20.1 %all-reduce.13.cloned.1.call-done = (f32[64,135]{0,1:T(8,128)}, f32[5,1728]{1,0:T(8,128)}) async-done(((f32[64,135]{0,1:T(8,128)}, f32[5,1728]{1,0:T(8,128)}), (f32[64,135]{0,1:T(8,128)}, f32[5,1728]{1,0:T(8,128)})) %all-reduce.13.cloned.1.call-update) | async-done | bytes 69136 | tf_op jit(solution)/shard_map/psum | solution.py:266
  405.7 38.0 %all-reduce.7.cloned.1.call-done = f32[64,1728]{0,1:T(8,128)} async-done(((f32[64,1728]{0,1:T(8,128)}), f32[64,1728]{0,1:T(8,128)}) %all-reduce.7.cloned.1.call-update) | async-done | bytes 442384 | tf_op jit(solution)/shard_map/psum | solution.py:266
  445.1 72.2 %all-reduce.11.cloned.1.call-done = (f32[64,135]{0,1:T(8,128)}, f32[5,1728]{1,0:T(8,128)}) async-done(((f32[64,135]{0,1:T(8,128)}, f32[5,1728]{1,0:T(8,128)}), (f32[64,135]{0,1:T(8,128)}, f32[5,1728]{1,0:T(8,128)})) %all-reduce.11.cloned.1.call-update) | async-done | bytes 69136 | tf_op jit(solution)/shard_map/psum | solution.py:266
  517.3 1.6 copy.1540
  518.9 77.7 %all-reduce.9.cloned.1.call-done = f32[64,1728]{0,1:T(8,128)} async-done(((f32[64,1728]{0,1:T(8,128)}), f32[64,1728]{0,1:T(8,128)}) %all-reduce.9.cloned.1.call-update) | async-done | bytes 442384 | tf_op jit(solution)/shard_map/psum | solution.py:266
  596.6 2.2 copy.1541
  (789 shorter events, 161.2 us)
Async XLA Ops:
  7.2 398.5 %all-reduce.13.cloned.1.call-start = ((), (), s32[]{:S(2)}) async-start(), calls=%async_computation.3 | async-start | bytes 253952 | tf_op jit(solution)/shard_map/psum | solution.py:266
  8.0 21.2 %collective-permute-start.1 = (f32[5,3,8,8]{3,2,1,0:T(8,128)S(1)}, f32[5,3,8,8]{3,2,1,0:T(8,128)S(1)}, u32[]{:S(2)}, u32[]{:S(2)}) collective-permute-start(f32[5,3,8,8]{3,2,1,0:T(8,128)S(1)} %get-tuple-element.275), channel_id=1, source_target_pairs={{0,8},{8,16},{16,24},{1,9},{9,17},{17,25},{2,10},{10,18},{18,26},{... | collective-permute-start | bytes 11528 | tf_op jit(solution)/shard_map/ppermute | solution.py:21
  10.5 19.8 %collective-permute-start = (f32[5,3,8,8]{3,2,1,0:T(8,128)S(1)}, f32[5,3,8,8]{3,2,1,0:T(8,128)S(1)}, u32[]{:S(2)}, u32[]{:S(2)}) collective-permute-start(f32[5,3,8,8]{3,2,1,0:T(8,128)S(1)} %get-tuple-element.274), channel_id=1, source_target_pairs={{8,0},{16,8},{24,16},{9,1},{17,9},{25,17},{10,2},{18,10},{26,18},{... | collective-permute-start | bytes 11528 | tf_op jit(solution)/shard_map/ppermute | solution.py:23
  13.1 21.9 %collective-permute-start.24 = (f32[8,3,8,8]{3,2,1,0:T(8,128)S(1)}, f32[8,3,8,8]{3,2,1,0:T(8,128)S(1)}, u32[]{:S(2)}, u32[]{:S(2)}) collective-permute-start(f32[8,3,8,8]{3,2,1,0:T(8,128)S(1)} %get-tuple-element.204), channel_id=1, source_target_pairs={{8,0},{16,8},{24,16},{9,1},{17,9},{25,17},{10,2},{18,10},{26,18},{... | collective-permute-start | bytes 18440 | tf_op jit(solution)/shard_map/ppermute | solution.py:23
  14.4 20.6 %collective-permute-start.25 = (f32[8,3,8,8]{3,2,1,0:T(8,128)S(1)}, f32[8,3,8,8]{3,2,1,0:T(8,128)S(1)}, u32[]{:S(2)}, u32[]{:S(2)}) collective-permute-start(f32[8,3,8,8]{3,2,1,0:T(8,128)S(1)} %get-tuple-element.203), channel_id=1, source_target_pairs={{0,8},{8,16},{16,24},{1,9},{9,17},{17,25},{2,10},{10,18},{18,26},{... | collective-permute-start | bytes 18440 | tf_op jit(solution)/shard_map/ppermute | solution.py:21
  30.3 12.2 %collective-permute-start.3 = (f32[5,10,3,8]{3,2,1,0:T(4,128)S(1)}, f32[5,10,3,8]{3,2,1,0:T(4,128)S(1)}, u32[]{:S(2)}, u32[]{:S(2)}) collective-permute-start(f32[5,10,3,8]{3,2,1,0:T(4,128)S(1)} %get-tuple-element.155), channel_id=1, source_target_pairs={{0,1},{1,2},{2,3},{3,4},{4,5},{5,6},{6,7},{8,9},{9,10},{10,11},{11... | collective-permute-start | bytes 14408 | tf_op jit(solution)/shard_map/ppermute | solution.py:21
  33.7 8.7 %collective-permute-start.2 = (f32[5,10,3,8]{3,2,1,0:T(4,128)S(1)}, f32[5,10,3,8]{3,2,1,0:T(4,128)S(1)}, u32[]{:S(2)}, u32[]{:S(2)}) collective-permute-start(f32[5,10,3,8]{3,2,1,0:T(4,128)S(1)} %get-tuple-element.154), channel_id=1, source_target_pairs={{1,0},{2,1},{3,2},{4,3},{5,4},{6,5},{7,6},{9,8},{10,9},{11,10},{12... | collective-permute-start | bytes 14408 | tf_op jit(solution)/shard_map/ppermute | solution.py:23
  35.9 27.0 %collective-permute-start.27 = (f32[8,10,3,8]{3,2,1,0:T(4,128)}, f32[8,10,3,8]{3,2,1,0:T(4,128)}, u32[]{:S(2)}, u32[]{:S(2)}) collective-permute-start(f32[8,10,3,8]{3,2,1,0:T(4,128)} %get-tuple-element.97), channel_id=1, source_target_pairs={{0,1},{1,2},{2,3},{3,4},{4,5},{5,6},{6,7},{8,9},{9,10},{10,11},{11... | collective-permute-start | bytes 23048 | tf_op jit(solution)/shard_map/ppermute | solution.py:21
  41.1 21.8 %collective-permute-start.26 = (f32[8,10,3,8]{3,2,1,0:T(4,128)}, f32[8,10,3,8]{3,2,1,0:T(4,128)}, u32[]{:S(2)}, u32[]{:S(2)}) collective-permute-start(f32[8,10,3,8]{3,2,1,0:T(4,128)} %get-tuple-element.96), channel_id=1, source_target_pairs={{1,0},{2,1},{3,2},{4,3},{5,4},{6,5},{7,6},{9,8},{10,9},{11,10},{12... | collective-permute-start | bytes 23048 | tf_op jit(solution)/shard_map/ppermute | solution.py:23
  64.0 5.4 collective-permute-start.28
  70.2 7.4 %collective-permute-start.31 = (f32[8,10,3,8]{3,2,1,0:T(4,128)S(1)}, f32[8,10,3,8]{3,2,1,0:T(4,128)S(1)}, u32[]{:S(2)}, u32[]{:S(2)}) collective-permute-start(f32[8,10,3,8]{3,2,1,0:T(4,128)S(1)} %get-tuple-element.95), channel_id=1, source_target_pairs={{0,1},{1,2},{2,3},{3,4},{4,5},{5,6},{6,7},{8,9},{9,10},{10,11},{11... | collective-permute-start | bytes 23048 | tf_op jit(solution)/shard_map/ppermute | solution.py:21
  74.5 8.1 %collective-permute-start.30 = (f32[8,10,3,8]{3,2,1,0:T(4,128)S(1)}, f32[8,10,3,8]{3,2,1,0:T(4,128)S(1)}, u32[]{:S(2)}, u32[]{:S(2)}) collective-permute-start(f32[8,10,3,8]{3,2,1,0:T(4,128)S(1)} %get-tuple-element.94), channel_id=1, source_target_pairs={{1,0},{2,1},{3,2},{4,3},{5,4},{6,5},{7,6},{9,8},{10,9},{11,10},{12... | collective-permute-start | bytes 23048 | tf_op jit(solution)/shard_map/ppermute | solution.py:23
  85.1 28.6 %collective-permute-start.5 = (f32[5,3,8,8]{3,2,1,0:T(8,128)S(1)}, f32[5,3,8,8]{3,2,1,0:T(8,128)S(1)}, u32[]{:S(2)}, u32[]{:S(2)}) collective-permute-start(f32[5,3,8,8]{3,2,1,0:T(8,128)S(1)} %get-tuple-element.266), channel_id=1, source_target_pairs={{0,8},{8,16},{16,24},{1,9},{9,17},{17,25},{2,10},{10,18},{18,26},{... | collective-permute-start | bytes 11528 | tf_op jit(solution)/shard_map/ppermute | solution.py:21
  88.4 25.4 %collective-permute-start.4 = (f32[5,3,8,8]{3,2,1,0:T(8,128)S(1)}, f32[5,3,8,8]{3,2,1,0:T(8,128)S(1)}, u32[]{:S(2)}, u32[]{:S(2)}) collective-permute-start(f32[5,3,8,8]{3,2,1,0:T(8,128)S(1)} %get-tuple-element.267), channel_id=1, source_target_pairs={{8,0},{16,8},{24,16},{9,1},{17,9},{25,17},{10,2},{18,10},{26,18},{... | collective-permute-start | bytes 11528 | tf_op jit(solution)/shard_map/ppermute | solution.py:23
  89.7 30.3 %collective-permute-start.40 = (f32[8,3,8,8]{3,2,1,0:T(8,128)S(1)}, f32[8,3,8,8]{3,2,1,0:T(8,128)S(1)}, u32[]{:S(2)}, u32[]{:S(2)}) collective-permute-start(f32[8,3,8,8]{3,2,1,0:T(8,128)S(1)} %get-tuple-element.194), channel_id=1, source_target_pairs={{8,0},{16,8},{24,16},{9,1},{17,9},{25,17},{10,2},{18,10},{26,18},{... | collective-permute-start | bytes 18440 | tf_op jit(solution)/shard_map/ppermute | solution.py:23
  91.1 8.9 %collective-permute-start.33 = (bf16[5,1,8,8]{3,2,1,0:T(8,128)(2,1)S(1)}, bf16[5,1,8,8]{3,2,1,0:T(8,128)(2,1)S(1)}, u32[]{:S(2)}, u32[]{:S(2)}) collective-permute-start(bf16[5,1,8,8]{3,2,1,0:T(8,128)(2,1)S(1)} %get-tuple-element.305), channel_id=1, source_target_pairs={{8,0},{16,8},{24,16},{9,1},{17,9},{25,17},{10,2},{18,10},{26,18},{... | collective-permute-start | bytes 1928 | tf_op jit(solution)/shard_map/ppermute | solution.py:23
  92.4 7.9 %collective-permute-start.32 = (bf16[5,1,8,8]{3,2,1,0:T(8,128)(2,1)S(1)}, bf16[5,1,8,8]{3,2,1,0:T(8,128)(2,1)S(1)}, u32[]{:S(2)}, u32[]{:S(2)}) collective-permute-start(bf16[5,1,8,8]{3,2,1,0:T(8,128)(2,1)S(1)} %get-tuple-element.304), channel_id=1, source_target_pairs={{0,8},{8,16},{16,24},{1,9},{9,17},{17,25},{2,10},{10,18},{18,26},{... | collective-permute-start | bytes 1928 | tf_op jit(solution)/shard_map/ppermute | solution.py:21
  100.3 6.8 %collective-permute-start.35 = (bf16[5,6,1,8]{3,2,1,0:T(2,128)(2,1)S(1)}, bf16[5,6,1,8]{3,2,1,0:T(2,128)(2,1)S(1)}, u32[]{:S(2)}, u32[]{:S(2)}) collective-permute-start(bf16[5,6,1,8]{3,2,1,0:T(2,128)(2,1)S(1)} %get-tuple-element.287), channel_id=1, source_target_pairs={{1,0},{2,1},{3,2},{4,3},{5,4},{6,5},{7,6},{9,8},{10,9},{11,10},{12... | collective-permute-start | bytes 1448 | tf_op jit(solution)/shard_map/ppermute | solution.py:23
  101.6 9.4 %collective-permute-start.34 = (bf16[5,6,1,8]{3,2,1,0:T(2,128)(2,1)S(1)}, bf16[5,6,1,8]{3,2,1,0:T(2,128)(2,1)S(1)}, u32[]{:S(2)}, u32[]{:S(2)}) collective-permute-start(bf16[5,6,1,8]{3,2,1,0:T(2,128)(2,1)S(1)} %get-tuple-element.286), channel_id=1, source_target_pairs={{0,1},{1,2},{2,3},{3,4},{4,5},{5,6},{6,7},{8,9},{9,10},{10,11},{11... | collective-permute-start | bytes 1448 | tf_op jit(solution)/shard_map/ppermute | solution.py:21
  107.7 12.3 %collective-permute-start.41 = (f32[8,3,8,8]{3,2,1,0:T(8,128)S(1)}, f32[8,3,8,8]{3,2,1,0:T(8,128)S(1)}, u32[]{:S(2)}, u32[]{:S(2)}) collective-permute-start(f32[8,3,8,8]{3,2,1,0:T(8,128)S(1)} %get-tuple-element.193), channel_id=1, source_target_pairs={{0,8},{8,16},{16,24},{1,9},{9,17},{17,25},{2,10},{10,18},{18,26},{... | collective-permute-start | bytes 18440 | tf_op jit(solution)/shard_map/ppermute | solution.py:21
  113.8 12.2 %collective-permute-start.7 = (f32[5,10,3,8]{3,2,1,0:T(4,128)S(1)}, f32[5,10,3,8]{3,2,1,0:T(4,128)S(1)}, u32[]{:S(2)}, u32[]{:S(2)}) collective-permute-start(f32[5,10,3,8]{3,2,1,0:T(4,128)S(1)} %get-tuple-element.151), channel_id=1, source_target_pairs={{0,1},{1,2},{2,3},{3,4},{4,5},{5,6},{6,7},{8,9},{9,10},{10,11},{11... | collective-permute-start | bytes 14408 | tf_op jit(solution)/shard_map/ppermute | solution.py:21
  118.4 7.7 %collective-permute-start.6 = (f32[5,10,3,8]{3,2,1,0:T(4,128)S(1)}, f32[5,10,3,8]{3,2,1,0:T(4,128)S(1)}, u32[]{:S(2)}, u32[]{:S(2)}) collective-permute-start(f32[5,10,3,8]{3,2,1,0:T(4,128)S(1)} %get-tuple-element.150), channel_id=1, source_target_pairs={{1,0},{2,1},{3,2},{4,3},{5,4},{6,5},{7,6},{9,8},{10,9},{11,10},{12... | collective-permute-start | bytes 14408 | tf_op jit(solution)/shard_map/ppermute | solution.py:23
  120.1 20.9 %collective-permute-start.43 = (f32[8,10,3,8]{3,2,1,0:T(4,128)S(1)}, f32[8,10,3,8]{3,2,1,0:T(4,128)S(1)}, u32[]{:S(2)}, u32[]{:S(2)}) collective-permute-start(f32[8,10,3,8]{3,2,1,0:T(4,128)S(1)} %get-tuple-element.93), channel_id=1, source_target_pairs={{0,1},{1,2},{2,3},{3,4},{4,5},{5,6},{6,7},{8,9},{9,10},{10,11},{11... | collective-permute-start | bytes 23048 | tf_op jit(solution)/shard_map/ppermute | solution.py:21
  124.7 16.3 %collective-permute-start.42 = (f32[8,10,3,8]{3,2,1,0:T(4,128)S(1)}, f32[8,10,3,8]{3,2,1,0:T(4,128)S(1)}, u32[]{:S(2)}, u32[]{:S(2)}) collective-permute-start(f32[8,10,3,8]{3,2,1,0:T(4,128)S(1)} %get-tuple-element.92), channel_id=1, source_target_pairs={{1,0},{2,1},{3,2},{4,3},{5,4},{6,5},{7,6},{9,8},{10,9},{11,10},{12... | collective-permute-start | bytes 23048 | tf_op jit(solution)/shard_map/ppermute | solution.py:23
  126.4 5.7 collective-permute-start.9
  133.9 7.7 %collective-permute-start.11 = (f32[5,10,3,8]{3,2,1,0:T(4,128)S(1)}, f32[5,10,3,8]{3,2,1,0:T(4,128)S(1)}, u32[]{:S(2)}, u32[]{:S(2)}) collective-permute-start(f32[5,10,3,8]{3,2,1,0:T(4,128)S(1)} %get-tuple-element.149), channel_id=1, source_target_pairs={{0,1},{1,2},{2,3},{3,4},{4,5},{5,6},{6,7},{8,9},{9,10},{10,11},{11... | collective-permute-start | bytes 14408 | tf_op jit(solution)/shard_map/ppermute | solution.py:21
  139.4 7.5 %collective-permute-start.10 = (f32[5,10,3,8]{3,2,1,0:T(4,128)S(1)}, f32[5,10,3,8]{3,2,1,0:T(4,128)S(1)}, u32[]{:S(2)}, u32[]{:S(2)}) collective-permute-start(f32[5,10,3,8]{3,2,1,0:T(4,128)S(1)} %get-tuple-element.148), channel_id=1, source_target_pairs={{1,0},{2,1},{3,2},{4,3},{5,4},{6,5},{7,6},{9,8},{10,9},{11,10},{12... | collective-permute-start | bytes 14408 | tf_op jit(solution)/shard_map/ppermute | solution.py:23
  147.8 5.4 collective-permute-start.13
  155.3 11.4 %collective-permute-start.15 = (f32[5,10,3,8]{3,2,1,0:T(4,128)S(1)}, f32[5,10,3,8]{3,2,1,0:T(4,128)S(1)}, u32[]{:S(2)}, u32[]{:S(2)}) collective-permute-start(f32[5,10,3,8]{3,2,1,0:T(4,128)S(1)} %get-tuple-element.147), channel_id=1, source_target_pairs={{0,1},{1,2},{2,3},{3,4},{4,5},{5,6},{6,7},{8,9},{9,10},{10,11},{11... | collective-permute-start | bytes 14408 | tf_op jit(solution)/shard_map/ppermute | solution.py:21
  160.1 6.6 %collective-permute-start.14 = (f32[5,10,3,8]{3,2,1,0:T(4,128)S(1)}, f32[5,10,3,8]{3,2,1,0:T(4,128)S(1)}, u32[]{:S(2)}, u32[]{:S(2)}) collective-permute-start(f32[5,10,3,8]{3,2,1,0:T(4,128)S(1)} %get-tuple-element.146), channel_id=1, source_target_pairs={{1,0},{2,1},{3,2},{4,3},{5,4},{6,5},{7,6},{9,8},{10,9},{11,10},{12... | collective-permute-start | bytes 14408 | tf_op jit(solution)/shard_map/ppermute | solution.py:23
  180.0 24.7 %collective-permute-start.37 = (bf16[64,1,8,8]{0,3,2,1:T(8,128)(2,1)S(1)}, bf16[64,1,8,8]{0,3,2,1:T(8,128)(2,1)S(1)}, u32[]{:S(2)}, u32[]{:S(2)}) collective-permute-start(bf16[64,1,8,8]{0,3,2,1:T(8,128)(2,1)S(1)} %get-tuple-element.283), channel_id=1, source_target_pairs={{8,0},{16,8},{24,16},{9,1},{17,9},{25,17},{10,2},{18,10},{26,18},{... | collective-permute-start | bytes 24584 | tf_op jit(solution)/shard_map/ppermute | solution.py:23
  181.3 23.4 %collective-permute-start.36 = (bf16[64,1,8,8]{0,3,2,1:T(8,128)(2,1)S(1)}, bf16[64,1,8,8]{0,3,2,1:T(8,128)(2,1)S(1)}, u32[]{:S(2)}, u32[]{:S(2)}) collective-permute-start(bf16[64,1,8,8]{0,3,2,1:T(8,128)(2,1)S(1)} %get-tuple-element.282), channel_id=1, source_target_pairs={{0,8},{8,16},{16,24},{1,9},{9,17},{17,25},{2,10},{10,18},{18,26},{... | collective-permute-start | bytes 24584 | tf_op jit(solution)/shard_map/ppermute | solution.py:21
  205.4 7.6 %collective-permute-start.39 = (bf16[64,6,1,8]{0,3,2,1:T(8,128)(2,1)S(1)}, bf16[64,6,1,8]{0,3,2,1:T(8,128)(2,1)S(1)}, u32[]{:S(2)}, u32[]{:S(2)}) collective-permute-start(bf16[64,6,1,8]{0,3,2,1:T(8,128)(2,1)S(1)} %get-tuple-element.230), channel_id=1, source_target_pairs={{1,0},{2,1},{3,2},{4,3},{5,4},{6,5},{7,6},{9,8},{10,9},{11,10},{12... | collective-permute-start | bytes 18440 | tf_op jit(solution)/shard_map/ppermute | solution.py:23
  206.7 6.3 %collective-permute-start.38 = (bf16[64,6,1,8]{0,3,2,1:T(8,128)(2,1)S(1)}, bf16[64,6,1,8]{0,3,2,1:T(8,128)(2,1)S(1)}, u32[]{:S(2)}, u32[]{:S(2)}) collective-permute-start(bf16[64,6,1,8]{0,3,2,1:T(8,128)(2,1)S(1)} %get-tuple-element.229), channel_id=1, source_target_pairs={{0,1},{1,2},{2,3},{3,4},{4,5},{5,6},{6,7},{8,9},{9,10},{10,11},{11... | collective-permute-start | bytes 18440 | tf_op jit(solution)/shard_map/ppermute | solution.py:21
  214.1 17.3 %collective-permute-start.45 = (bf16[64,1,8,8]{0,3,2,1:T(8,128)(2,1)S(1)}, bf16[64,1,8,8]{0,3,2,1:T(8,128)(2,1)S(1)}, u32[]{:S(2)}, u32[]{:S(2)}) collective-permute-start(bf16[64,1,8,8]{0,3,2,1:T(8,128)(2,1)S(1)} %get-tuple-element.281), channel_id=1, source_target_pairs={{8,0},{16,8},{24,16},{9,1},{17,9},{25,17},{10,2},{18,10},{26,18},{... | collective-permute-start | bytes 24584 | tf_op jit(solution)/shard_map/ppermute | solution.py:23
  215.4 16.0 %collective-permute-start.44 = (bf16[64,1,8,8]{0,3,2,1:T(8,128)(2,1)S(1)}, bf16[64,1,8,8]{0,3,2,1:T(8,128)(2,1)S(1)}, u32[]{:S(2)}, u32[]{:S(2)}) collective-permute-start(bf16[64,1,8,8]{0,3,2,1:T(8,128)(2,1)S(1)} %get-tuple-element.280), channel_id=1, source_target_pairs={{0,8},{8,16},{16,24},{1,9},{9,17},{17,25},{2,10},{10,18},{18,26},{... | collective-permute-start | bytes 24584 | tf_op jit(solution)/shard_map/ppermute | solution.py:21
  231.4 6.5 %collective-permute-start.47 = (bf16[64,6,1,8]{0,3,2,1:T(8,128)(2,1)S(1)}, bf16[64,6,1,8]{0,3,2,1:T(8,128)(2,1)S(1)}, u32[]{:S(2)}, u32[]{:S(2)}) collective-permute-start(bf16[64,6,1,8]{0,3,2,1:T(8,128)(2,1)S(1)} %get-tuple-element.228), channel_id=1, source_target_pairs={{1,0},{2,1},{3,2},{4,3},{5,4},{6,5},{7,6},{9,8},{10,9},{11,10},{12... | collective-permute-start | bytes 18440 | tf_op jit(solution)/shard_map/ppermute | solution.py:23
  232.7 6.1 %collective-permute-start.46 = (bf16[64,6,1,8]{0,3,2,1:T(8,128)(2,1)S(1)}, bf16[64,6,1,8]{0,3,2,1:T(8,128)(2,1)S(1)}, u32[]{:S(2)}, u32[]{:S(2)}) collective-permute-start(bf16[64,6,1,8]{0,3,2,1:T(8,128)(2,1)S(1)} %get-tuple-element.227), channel_id=1, source_target_pairs={{0,1},{1,2},{2,3},{3,4},{4,5},{5,6},{6,7},{8,9},{9,10},{10,11},{11... | collective-permute-start | bytes 18440 | tf_op jit(solution)/shard_map/ppermute | solution.py:21
  242.9 5.3 collective-permute-start.48
  244.2 4.7 collective-permute-start.49
  249.0 7.7 %collective-permute-start.51 = (f32[8,10,3,8]{3,2,1,0:T(4,128)S(1)}, f32[8,10,3,8]{3,2,1,0:T(4,128)S(1)}, u32[]{:S(2)}, u32[]{:S(2)}) collective-permute-start(f32[8,10,3,8]{3,2,1,0:T(4,128)S(1)} %get-tuple-element.91), channel_id=1, source_target_pairs={{0,1},{1,2},{2,3},{3,4},{4,5},{5,6},{6,7},{8,9},{9,10},{10,11},{11... | collective-permute-start | bytes 23048 | tf_op jit(solution)/shard_map/ppermute | solution.py:21
  253.5 8.4 %collective-permute-start.50 = (f32[8,10,3,8]{3,2,1,0:T(4,128)S(1)}, f32[8,10,3,8]{3,2,1,0:T(4,128)S(1)}, u32[]{:S(2)}, u32[]{:S(2)}) collective-permute-start(f32[8,10,3,8]{3,2,1,0:T(4,128)S(1)} %get-tuple-element.90), channel_id=1, source_target_pairs={{1,0},{2,1},{3,2},{4,3},{5,4},{6,5},{7,6},{9,8},{10,9},{11,10},{12... | collective-permute-start | bytes 23048 | tf_op jit(solution)/shard_map/ppermute | solution.py:23
  263.9 19.7 %collective-permute-start.52 = (f32[8,3,8,8]{3,2,1,0:T(8,128)S(1)}, f32[8,3,8,8]{3,2,1,0:T(8,128)S(1)}, u32[]{:S(2)}, u32[]{:S(2)}) collective-permute-start(f32[8,3,8,8]{3,2,1,0:T(8,128)S(1)} %get-tuple-element.184), channel_id=1, source_target_pairs={{8,0},{16,8},{24,16},{9,1},{17,9},{25,17},{10,2},{18,10},{26,18},{... | collective-permute-start | bytes 18440 | tf_op jit(solution)/shard_map/ppermute | solution.py:23
  265.2 18.4 %collective-permute-start.53 = (f32[8,3,8,8]{3,2,1,0:T(8,128)S(1)}, f32[8,3,8,8]{3,2,1,0:T(8,128)S(1)}, u32[]{:S(2)}, u32[]{:S(2)}) collective-permute-start(f32[8,3,8,8]{3,2,1,0:T(8,128)S(1)} %get-tuple-element.183), channel_id=1, source_target_pairs={{0,8},{8,16},{16,24},{1,9},{9,17},{17,25},{2,10},{10,18},{18,26},{... | collective-permute-start | bytes 18440 | tf_op jit(solution)/shard_map/ppermute | solution.py:21
  269.0 6.9 %collective-permute-start.17 = (f32[5,3,8,8]{3,2,1,0:T(8,128)S(1)}, f32[5,3,8,8]{3,2,1,0:T(8,128)S(1)}, u32[]{:S(2)}, u32[]{:S(2)}) collective-permute-start(f32[5,3,8,8]{3,2,1,0:T(8,128)S(1)} %get-tuple-element.248), channel_id=1, source_target_pairs={{0,8},{8,16},{16,24},{1,9},{9,17},{17,25},{2,10},{10,18},{18,26},{... | collective-permute-start | bytes 11528 | tf_op jit(solution)/shard_map/ppermute | solution.py:21
  277.1 13.1 %collective-permute-start.19 = (f32[5,10,3,8]{3,2,1,0:T(4,128)S(1)}, f32[5,10,3,8]{3,2,1,0:T(4,128)S(1)}, u32[]{:S(2)}, u32[]{:S(2)}) collective-permute-start(f32[5,10,3,8]{3,2,1,0:T(4,128)S(1)} %get-tuple-element.143), channel_id=1, source_target_pairs={{0,1},{1,2},{2,3},{3,4},{4,5},{5,6},{6,7},{8,9},{9,10},{10,11},{11... | collective-permute-start | bytes 14408 | tf_op jit(solution)/shard_map/ppermute | solution.py:21
  282.0 8.3 %collective-permute-start.18 = (f32[5,10,3,8]{3,2,1,0:T(4,128)S(1)}, f32[5,10,3,8]{3,2,1,0:T(4,128)S(1)}, u32[]{:S(2)}, u32[]{:S(2)}) collective-permute-start(f32[5,10,3,8]{3,2,1,0:T(4,128)S(1)} %get-tuple-element.142), channel_id=1, source_target_pairs={{1,0},{2,1},{3,2},{4,3},{5,4},{6,5},{7,6},{9,8},{10,9},{11,10},{12... | collective-permute-start | bytes 14408 | tf_op jit(solution)/shard_map/ppermute | solution.py:23
  283.7 7.8 %collective-permute-start.55 = (f32[8,10,3,8]{3,2,1,0:T(4,128)S(1)}, f32[8,10,3,8]{3,2,1,0:T(4,128)}, u32[]{:S(2)}, u32[]{:S(2)}) collective-permute-start(f32[8,10,3,8]{3,2,1,0:T(4,128)S(1)} %get-tuple-element.89), channel_id=1, source_target_pairs={{0,1},{1,2},{2,3},{3,4},{4,5},{5,6},{6,7},{8,9},{9,10},{10,11},{11... | collective-permute-start | bytes 23048 | tf_op jit(solution)/shard_map/ppermute | solution.py:21
  288.9 8.0 %collective-permute-start.54 = (f32[8,10,3,8]{3,2,1,0:T(4,128)S(1)}, f32[8,10,3,8]{3,2,1,0:T(4,128)}, u32[]{:S(2)}, u32[]{:S(2)}) collective-permute-start(f32[8,10,3,8]{3,2,1,0:T(4,128)S(1)} %get-tuple-element.88), channel_id=1, source_target_pairs={{1,0},{2,1},{3,2},{4,3},{5,4},{6,5},{7,6},{9,8},{10,9},{11,10},{12... | collective-permute-start | bytes 23048 | tf_op jit(solution)/shard_map/ppermute | solution.py:23
  299.9 71.6 %collective-permute-start.21 = (f32[5,3,8,8]{3,2,1,0:T(8,128)}, f32[5,3,8,8]{3,2,1,0:T(8,128)S(1)}, u32[]{:S(2)}, u32[]{:S(2)}) collective-permute-start(f32[5,3,8,8]{3,2,1,0:T(8,128)} %get-tuple-element.245), channel_id=1, source_target_pairs={{0,8},{8,16},{16,24},{1,9},{9,17},{17,25},{2,10},{10,18},{18,26},{... | collective-permute-start | bytes 11528 | tf_op jit(solution)/shard_map/ppermute | solution.py:21
  302.7 68.8 %collective-permute-start.20 = (f32[5,3,8,8]{3,2,1,0:T(8,128)}, f32[5,3,8,8]{3,2,1,0:T(8,128)S(1)}, u32[]{:S(2)}, u32[]{:S(2)}) collective-permute-start(f32[5,3,8,8]{3,2,1,0:T(8,128)} %get-tuple-element.244), channel_id=1, source_target_pairs={{8,0},{16,8},{24,16},{9,1},{17,9},{25,17},{10,2},{18,10},{26,18},{... | collective-permute-start | bytes 11528 | tf_op jit(solution)/shard_map/ppermute | solution.py:23
  304.3 13.8 %collective-permute-start.57 = (bf16[5,1,8,8]{3,2,1,0:T(8,128)(2,1)S(1)}, bf16[5,1,8,8]{3,2,1,0:T(8,128)(2,1)S(1)}, u32[]{:S(2)}, u32[]{:S(2)}) collective-permute-start(bf16[5,1,8,8]{3,2,1,0:T(8,128)(2,1)S(1)} %get-tuple-element.303), channel_id=1, source_target_pairs={{8,0},{16,8},{24,16},{9,1},{17,9},{25,17},{10,2},{18,10},{26,18},{... | collective-permute-start | bytes 1928 | tf_op jit(solution)/shard_map/ppermute | solution.py:23
  305.6 12.5 %collective-permute-start.56 = (bf16[5,1,8,8]{3,2,1,0:T(8,128)(2,1)S(1)}, bf16[5,1,8,8]{3,2,1,0:T(8,128)(2,1)S(1)}, u32[]{:S(2)}, u32[]{:S(2)}) collective-permute-start(bf16[5,1,8,8]{3,2,1,0:T(8,128)(2,1)S(1)} %get-tuple-element.302), channel_id=1, source_target_pairs={{0,8},{8,16},{16,24},{1,9},{9,17},{17,25},{2,10},{10,18},{18,26},{... | collective-permute-start | bytes 1928 | tf_op jit(solution)/shard_map/ppermute | solution.py:21
  318.1 6.8 %collective-permute-start.59 = (bf16[5,6,1,8]{3,2,1,0:T(2,128)(2,1)S(1)}, bf16[5,6,1,8]{3,2,1,0:T(2,128)(2,1)S(1)}, u32[]{:S(2)}, u32[]{:S(2)}) collective-permute-start(bf16[5,6,1,8]{3,2,1,0:T(2,128)(2,1)S(1)} %get-tuple-element.285), channel_id=1, source_target_pairs={{1,0},{2,1},{3,2},{4,3},{5,4},{6,5},{7,6},{9,8},{10,9},{11,10},{12... | collective-permute-start | bytes 1448 | tf_op jit(solution)/shard_map/ppermute | solution.py:23
  319.4 6.0 collective-permute-start.58
  328.1 10.7 %collective-permute-start.61 = (bf16[64,1,8,8]{0,3,2,1:T(8,128)(2,1)S(1)}, bf16[64,1,8,8]{0,3,2,1:T(8,128)(2,1)S(1)}, u32[]{:S(2)}, u32[]{:S(2)}) collective-permute-start(bf16[64,1,8,8]{0,3,2,1:T(8,128)(2,1)S(1)} %get-tuple-element.279), channel_id=1, source_target_pairs={{8,0},{16,8},{24,16},{9,1},{17,9},{25,17},{10,2},{18,10},{26,18},{... | collective-permute-start | bytes 24584 | tf_op jit(solution)/shard_map/ppermute | solution.py:23
  329.4 9.4 %collective-permute-start.60 = (bf16[64,1,8,8]{0,3,2,1:T(8,128)(2,1)S(1)}, bf16[64,1,8,8]{0,3,2,1:T(8,128)(2,1)S(1)}, u32[]{:S(2)}, u32[]{:S(2)}) collective-permute-start(bf16[64,1,8,8]{0,3,2,1:T(8,128)(2,1)S(1)} %get-tuple-element.278), channel_id=1, source_target_pairs={{0,8},{8,16},{16,24},{1,9},{9,17},{17,25},{2,10},{10,18},{18,26},{... | collective-permute-start | bytes 24584 | tf_op jit(solution)/shard_map/ppermute | solution.py:21
  338.9 6.2 %collective-permute-start.63 = (bf16[64,6,1,8]{0,3,2,1:T(8,128)(2,1)S(1)}, bf16[64,6,1,8]{0,3,2,1:T(8,128)(2,1)S(1)}, u32[]{:S(2)}, u32[]{:S(2)}) collective-permute-start(bf16[64,6,1,8]{0,3,2,1:T(8,128)(2,1)S(1)} %get-tuple-element.226), channel_id=1, source_target_pairs={{1,0},{2,1},{3,2},{4,3},{5,4},{6,5},{7,6},{9,8},{10,9},{11,10},{12... | collective-permute-start | bytes 18440 | tf_op jit(solution)/shard_map/ppermute | solution.py:23
  340.2 6.1 %collective-permute-start.62 = (bf16[64,6,1,8]{0,3,2,1:T(8,128)(2,1)S(1)}, bf16[64,6,1,8]{0,3,2,1:T(8,128)(2,1)S(1)}, u32[]{:S(2)}, u32[]{:S(2)}) collective-permute-start(bf16[64,6,1,8]{0,3,2,1:T(8,128)(2,1)S(1)} %get-tuple-element.225), channel_id=1, source_target_pairs={{0,1},{1,2},{2,3},{3,4},{4,5},{5,6},{6,7},{8,9},{9,10},{10,11},{11... | collective-permute-start | bytes 18440 | tf_op jit(solution)/shard_map/ppermute | solution.py:21
  369.3 74.4 %all-reduce.7.cloned.1.call-start = ((), (), s32[]{:S(2)}) async-start(), calls=%async_computation | async-start | bytes 1769472 | tf_op jit(solution)/shard_map/psum | solution.py:266
  371.4 145.9 %all-reduce.11.cloned.1.call-start = ((), (), s32[]{:S(2)}) async-start(), calls=%async_computation.2 | async-start | bytes 253952 | tf_op jit(solution)/shard_map/psum | solution.py:266
  371.6 8.1 %collective-permute-start.23 = (f32[5,10,3,8]{3,2,1,0:T(4,128)S(1)}, f32[5,10,3,8]{3,2,1,0:T(4,128)S(1)}, u32[]{:S(2)}, u32[]{:S(2)}) collective-permute-start(f32[5,10,3,8]{3,2,1,0:T(4,128)S(1)} %get-tuple-element.141), channel_id=1, source_target_pairs={{0,1},{1,2},{2,3},{3,4},{4,5},{5,6},{6,7},{8,9},{9,10},{10,11},{11... | collective-permute-start | bytes 14408 | tf_op jit(solution)/shard_map/ppermute | solution.py:21
  376.5 8.4 %collective-permute-start.22 = (f32[5,10,3,8]{3,2,1,0:T(4,128)S(1)}, f32[5,10,3,8]{3,2,1,0:T(4,128)S(1)}, u32[]{:S(2)}, u32[]{:S(2)}) collective-permute-start(f32[5,10,3,8]{3,2,1,0:T(4,128)S(1)} %get-tuple-element.140), channel_id=1, source_target_pairs={{1,0},{2,1},{3,2},{4,3},{5,4},{6,5},{7,6},{9,8},{10,9},{11,10},{12... | collective-permute-start | bytes 14408 | tf_op jit(solution)/shard_map/ppermute | solution.py:23
  405.6 191.0 %all-reduce.9.cloned.1.call-start = ((), (), s32[]{:S(2)}) async-start(), calls=%async_computation.1 | async-start | bytes 1769472 | tf_op jit(solution)/shard_map/psum | solution.py:266
  (110 other events, 273.6 us)
Sparse Core Ops, SparseCore 0:
  369.4 36.1 all-reduce.12
  408.0 35.6 all-reduce.6
  447.1 70.1 all-reduce.10
  520.6 75.9 all-reduce.8
